TPU v7x, 32 devices: a whole 2x2x4 slice. The times are simulated.
32 devices in a mesh: clip: 8 (over z, x), row: 4 (over y, core).
Axes of the slice: x: 2, y: 2, z: 4, core: 2. Of those that a mesh axis runs over, the one named last changes fastest.
Arguments:
- features: bfloat16 [8, 128, 32, 256], P('clip', None, 'row'), may hold values from -6 to 6
- out_weight: bfloat16 [3, 128, 3, 3], replicated, may hold values from -0.1875 to 0.1875
- out_bias: float32 [3], replicated, may hold values from -0.5 to 0.5
- targets: bfloat16 [8, 3, 32, 256], P('clip', None, 'row'), may hold values from -1 to 1
- weight_one: bfloat16 [64, 3, 3, 3], replicated, may hold values from -1.25 to 1.25
- bias_one: float32 [64], replicated, may hold values from -0.2 to 0.2
- weight_two: bfloat16 [64, 64, 3, 3], replicated, may hold values from -0.375 to 0.375
- bias_two: float32 [64], replicated, may hold values from -0.2 to 0.2
- weight_three: bfloat16 [128, 64, 3, 3], replicated, may hold values from -0.375 to 0.375
- bias_three: float32 [128], replicated, may hold values from -0.2 to 0.2
- weight_four: bfloat16 [128, 128, 3, 3], replicated, may hold values from -0.25 to 0.25
- bias_four: float32 [128], replicated, may hold values from -0.2 to 0.2
- lin_one: float32 [64], replicated, may hold values from 0.05 to 0.5
- lin_two: float32 [128], replicated, may hold values from 0.05 to 0.5
Outputs:
- loss: float32 [], replicated
- feature_grad: bfloat16 [8, 128, 32, 256], P('clip', None, 'row')
- out_weight_grad: float32 [3, 128, 3, 3], replicated
- out_bias_grad: float32 [3], replicated
All inputs are finite; a program needn't handle non-finite values.
Results may differ from a plain program's by a relative error of at most 0.02.
Values may be sent and summed in bfloat16 or wider, within the bound.
A program may use at most 64 MiB of HBM per device.

v0:
```python
import math
import jax
import jax.numpy as jnp
from jax import lax
from jax.sharding import PartitionSpec as P

shift_values = [-0.03, -0.088, -0.188]
scale_values = [0.458, 0.448, 0.45]


def padded_2(array, sides, width):
    for axis, dim in sides:
        size, length = (lax.axis_size(axis), array.shape[dim])
        up = [(i, (i + 1) % size) for i in range(size - 1)]
        down = [(j, i) for i, j in up]
        last = lax.slice_in_dim(array, length - width, length, axis=dim)
        leading = lax.slice_in_dim(array, 0, width, axis=dim)
        before = lax.ppermute(last, axis, up)
        after = lax.ppermute(leading, axis, down)
        array = jnp.concatenate([before, array, after], axis=dim)
    return array


def shifted(array, axis, by):
    size = lax.axis_size(axis)
    pairs = [(i, i + by) for i in range(size) if 0 <= i + by < size]
    return lax.ppermute(array, axis, pairs)


def shift_array():
    return jnp.array(shift_values, jnp.float32).reshape(1, 3, 1, 1)


def scale_array():
    return jnp.array(scale_values, jnp.float32).reshape(1, 3, 1, 1)


def gelu_exact(values):
    return values * 0.5 * (1.0 + jax.scipy.special.erf(values / math.sqrt(2.0)))


def gelu_slope(values):
    normal_cdf = 0.5 * (1.0 + jax.scipy.special.erf(values / math.sqrt(2.0)))
    density = jnp.exp(-0.5 * values * values) / math.sqrt(2.0 * math.pi)
    return normal_cdf + values * density


def pad_rows(inputs):
    return jnp.pad(inputs, ((0, 0), (0, 0), (1, 1), (0, 0)))


def flipped(weight):
    return jnp.flip(weight, (2, 3)).transpose(1, 0, 2, 3)


def conv_valid(padded, weight):
    frame_count, channels, row_total, col_count = padded.shape
    row_count = row_total - 2
    outputs = weight.shape[0]
    wide = jnp.pad(padded, ((0, 0), (0, 0), (0, 0), (1, 1)))
    total = jnp.zeros((outputs, row_count * col_count), jnp.float32)
    for row_shift in range(3):
        for col_shift in range(3):
            piece = wide[0, :, row_shift : row_shift + row_count, col_shift : col_shift + col_count]
            total = total + jnp.dot(
                weight[:, :, row_shift, col_shift],
                piece.reshape(channels, row_count * col_count),
                preferred_element_type=jnp.float32,
            )
    results = [total.reshape(outputs, row_count, col_count)]
    return jnp.stack(results)


def grad_from_output(inputs, grad_pad):
    frame_count, channels, row_count, col_count = inputs.shape
    outputs = grad_pad.shape[1]
    wide = jnp.pad(grad_pad, ((0, 0), (0, 0), (0, 0), (1, 1)))
    blocks = []
    for row_shift in range(3):
        for col_shift in range(3):
            left = wide[
                0,
                :,
                2 - row_shift : 2 - row_shift + row_count,
                2 - col_shift : 2 - col_shift + col_count,
            ].reshape(outputs, row_count * col_count)
            right = inputs[0].reshape(channels, row_count * col_count)
            total = lax.dot_general(
                left, right, (((1,), (1,)), ((), ())), preferred_element_type=jnp.float32
            )
            blocks.append(total)
    return jnp.stack(blocks).reshape(3, 3, outputs, channels).transpose(2, 3, 0, 1)


def edge_terms(row_values, kernel_row):
    col_count = row_values.shape[2]
    wide = jnp.pad(row_values, ((0, 0), (0, 0), (1, 1)))
    total = jnp.zeros((row_values.shape[0], kernel_row.shape[0], col_count), jnp.float32)
    for col_shift in range(3):
        total = total + jnp.einsum(
            "oc,fcw->fow",
            kernel_row[:, :, col_shift],
            wide[:, :, col_shift : col_shift + col_count],
            preferred_element_type=jnp.float32,
        )
    return total


def pool_mean(values):
    frame_count, channels, row_count, col_count = values.shape
    return values.reshape(frame_count, channels, row_count // 2, 2, col_count // 2, 2).mean(
        axis=(3, 5)
    )


def upsample(values):
    return jnp.repeat(jnp.repeat(values, 2, 2), 2, 3)


def vgg_forward(image, weights):
    weight_one, bias_one, weight_two, bias_two, weight_three, bias_three, weight_four, bias_four = (
        weights
    )
    image_pad = padded_2(image, (("row", 2),), 1)
    pre_one = conv_valid(image_pad, weight_one) + bias_one[None, :, None, None]
    act_one = gelu_exact(pre_one).astype(jnp.bfloat16)
    act_pad = padded_2(act_one, (("row", 2),), 1)
    pre_two = conv_valid(act_pad, weight_two) + bias_two[None, :, None, None]
    act_two = gelu_exact(pre_two)
    pooled = pool_mean(act_two).astype(jnp.bfloat16)
    pooled_pad = padded_2(pooled, (("row", 2),), 1)
    pre_three = conv_valid(pooled_pad, weight_three) + bias_three[None, :, None, None]
    act_three = gelu_exact(pre_three).astype(jnp.bfloat16)
    three_pad = padded_2(act_three, (("row", 2),), 1)
    pre_four = conv_valid(three_pad, weight_four) + bias_four[None, :, None, None]
    act_four = gelu_exact(pre_four)
    return (pre_one, pre_two, act_two, pre_three, pre_four, act_four)


def lpips_layer(feat_dec, feat_tgt, lin, count):
    norm_dec = jnp.sqrt(jnp.sum(feat_dec * feat_dec, 1, keepdims=True) + 1e-06)
    norm_tgt = jnp.sqrt(jnp.sum(feat_tgt * feat_tgt, 1, keepdims=True) + 1e-06)
    unit_dec = feat_dec / norm_dec
    differ = unit_dec - feat_tgt / norm_tgt
    scaled = lin[None, :, None, None]
    part = jnp.sum(scaled * differ * differ) / count
    grad_unit = 2.0 * scaled * differ / count
    grad_feat = (grad_unit - unit_dec * jnp.sum(grad_unit * unit_dec, 1, keepdims=True)) / norm_dec
    return (part, grad_feat)


def local(
    features,
    out_weight,
    out_bias,
    targets,
    weight_one,
    bias_one,
    weight_two,
    bias_two,
    weight_three,
    bias_three,
    weight_four,
    bias_four,
    lin_one,
    lin_two,
):
    weights = (
        weight_one,
        bias_one,
        weight_two,
        bias_two,
        weight_three,
        bias_three,
        weight_four,
        bias_four,
    )
    row_count = features.shape[2]
    width = features.shape[3]
    height = row_count * lax.axis_size("row")
    pre_out = conv_valid(pad_rows(features), out_weight)
    down_terms = edge_terms(features[:, :, row_count - 1, :], out_weight[:, :, 0, :])
    up_terms = edge_terms(features[:, :, 0, :], out_weight[:, :, 2, :])
    from_above = shifted(down_terms, "row", 1)
    from_below = shifted(up_terms, "row", -1)
    pre_out = pre_out.at[:, :, 0, :].add(from_above)
    pre_out = pre_out.at[:, :, row_count - 1, :].add(from_below)
    decoded = (pre_out + out_bias[None, :, None, None]).astype(jnp.bfloat16)
    image_dec = ((decoded.astype(jnp.float32) - shift_array()) / scale_array()).astype(jnp.bfloat16)
    image_tgt = ((targets.astype(jnp.float32) - shift_array()) / scale_array()).astype(jnp.bfloat16)
    pre_one, pre_two, act_two, pre_three, pre_four, act_four = vgg_forward(image_dec, weights)
    tgt_acts = vgg_forward(image_tgt, weights)
    part_one, grad_two = lpips_layer(act_two, tgt_acts[2], lin_one, float(height * width))
    part_two, grad_four = lpips_layer(
        act_four, tgt_acts[5], lin_two, float(height // 2 * (width // 2))
    )
    grad_pre4 = (grad_four * gelu_slope(pre_four)).astype(jnp.bfloat16)
    grad_act3 = conv_valid(padded_2(grad_pre4, (("row", 2),), 1), flipped(weight_four))
    grad_pre3 = (grad_act3 * gelu_slope(pre_three)).astype(jnp.bfloat16)
    grad_pool = conv_valid(padded_2(grad_pre3, (("row", 2),), 1), flipped(weight_three))
    grad_pre2 = ((grad_two + 0.25 * upsample(grad_pool)) * gelu_slope(pre_two)).astype(jnp.bfloat16)
    grad_act1 = conv_valid(padded_2(grad_pre2, (("row", 2),), 1), flipped(weight_two))
    grad_pre1 = (grad_act1 * gelu_slope(pre_one)).astype(jnp.bfloat16)
    grad_image = conv_valid(padded_2(grad_pre1, (("row", 2),), 1), flipped(weight_one))
    grad_dec = (grad_image / scale_array()).astype(jnp.bfloat16)
    grad_pad = padded_2(grad_dec, (("row", 2),), 1)
    feature_grad = conv_valid(grad_pad, flipped(out_weight)).astype(jnp.bfloat16)
    weight_grad = grad_from_output(features, grad_pad)
    bias_grad = jnp.sum(grad_dec.astype(jnp.float32), (0, 2, 3))
    loss, weight_total, bias_total = lax.psum(
        (part_one + part_two, weight_grad, bias_grad), ("clip", "row")
    )
    return (loss, feature_grad, weight_total, bias_total)


def solution(mesh):
    placed = (
        P("clip", None, "row", None),
        P(),
        P(),
        P("clip", None, "row", None),
        P(),
        P(),
        P(),
        P(),
        P(),
        P(),
        P(),
        P(),
        P(),
        P(),
    )
    return jax.shard_map(
        local,
        mesh=mesh,
        in_specs=placed,
        out_specs=(P(), P("clip", None, "row", None), P(), P()),
        check_vma=False,
    )
```

profile of v0, /device:TPU:0, one launch (start us, length us, event | category | flops | bytes accessed | tf_op | source)
XLA Modules:
  0.0 208.2 jit_solution(6531382458531928736)
XLA Ops:
  3.4 2.4 %collective-permute-start = (f32[1,3,256]{2,1,0:T(4,128)S(1)}, f32[1,3,256]{2,1,0:T(4,128)S(1)}, u32[]{:S(2)}, u32[]{:S(2)}) collective-permute-start(f32[1,3,256]{2,1,0:T(4,128)S(1)} %fusion.18), channel_id=1, source_target_pairs={{0,1},{1,2},{2,3},{4,5},{5,6},{6,7},{8,9},{9,10},{10,11},{12,13},{... | collective-permute-start | bytes 9224 | tf_op jit(solution)/shard_map/ppermute | solution.py:27
  15.8 5.2 %collective-permute-start.2 = (bf16[1,3,1,256]{3,1,2,0:T(4,128)(2,1)S(1)}, bf16[1,3,1,256]{3,1,2,0:T(4,128)(2,1)S(1)}, u32[]{:S(2)}, u32[]{:S(2)}) collective-permute-start(bf16[1,3,1,256]{3,1,2,0:T(4,128)(2,1)S(1)} %get-tuple-element.202), channel_id=1, source_target_pairs={{0,1},{1,2},{2,3},{4,5},{5,6},{6,7},{8,9},{9,10},{10,11},{12,13},{... | collective-permute-start | bytes 4616 | tf_op jit(solution)/shard_map/ppermute | solution.py:18
  22.2 4.3 %collective-permute-start.6 = (bf16[1,3,1,256]{3,1,2,0:T(4,128)(2,1)S(1)}, bf16[1,3,1,256]{3,1,2,0:T(4,128)(2,1)S(1)}, u32[]{:S(2)}, u32[]{:S(2)}) collective-permute-start(bf16[1,3,1,256]{3,1,2,0:T(4,128)(2,1)S(1)} %get-tuple-element.198), channel_id=1, source_target_pairs={{0,1},{1,2},{2,3},{4,5},{5,6},{6,7},{8,9},{9,10},{10,11},{12,13},{... | collective-permute-start | bytes 4616 | tf_op jit(solution)/shard_map/ppermute | solution.py:18
  34.3 4.3 %collective-permute-start.8 = (bf16[1,64,1,256]{3,2,1,0:T(2,128)(2,1)S(1)}, bf16[1,64,1,256]{3,2,1,0:T(2,128)(2,1)S(1)}, u32[]{:S(2)}, u32[]{:S(2)}) collective-permute-start(bf16[1,64,1,256]{3,2,1,0:T(2,128)(2,1)S(1)} %get-tuple-element.108), channel_id=1, source_target_pairs={{0,1},{1,2},{2,3},{4,5},{5,6},{6,7},{8,9},{9,10},{10,11},{12,13},{... | collective-permute-start | bytes 98312 | tf_op jit(solution)/shard_map/ppermute | solution.py:18
  40.1 4.2 %collective-permute-start.4 = (bf16[1,64,1,256]{3,2,1,0:T(2,128)(2,1)S(1)}, bf16[1,64,1,256]{3,2,1,0:T(2,128)(2,1)S(1)}, u32[]{:S(2)}, u32[]{:S(2)}) collective-permute-start(bf16[1,64,1,256]{3,2,1,0:T(2,128)(2,1)S(1)} %get-tuple-element.112), channel_id=1, source_target_pairs={{0,1},{1,2},{2,3},{4,5},{5,6},{6,7},{8,9},{9,10},{10,11},{12,13},{... | collective-permute-start | bytes 98312 | tf_op jit(solution)/shard_map/ppermute | solution.py:18
  46.1 2.5 %collective-permute-done.5 = bf16[1,64,1,256]{3,2,1,0:T(2,128)(2,1)S(1)} collective-permute-done((bf16[1,64,1,256]{3,2,1,0:T(2,128)(2,1)S(1)}, bf16[1,64,1,256]{3,2,1,0:T(2,128)(2,1)S(1)}, u32[]{:S(2)}, u32[]{:S(2)}) %collective-permute-start.5) | collective-permute-done | bytes 32800 | tf_op jit(solution)/shard_map/ppermute | solution.py:19
  60.3 2.1 %copy.253 = f32[1,64,4,2,128,2]{4,1,5,3,2,0:T(8,128)} copy(f32[1,64,4,2,128,2]{1,5,4,3,2,0:T(2,128)} %bitcast.1069) | data formatting | bytes 1048576 | tf_op jit(solution)/shard_map/stack;reshape | solution.py:71
  62.5 2.1 multiply_reduce_fusion.2
  66.5 4.8 %collective-permute-start.14 = (bf16[1,64,1,128]{1,3,2,0:T(8,128)(2,1)S(1)}, bf16[1,64,1,128]{1,3,2,0:T(8,128)(2,1)S(1)}, u32[]{:S(2)}, u32[]{:S(2)}) collective-permute-start(bf16[1,64,1,128]{1,3,2,0:T(8,128)(2,1)S(1)} %get-tuple-element.172), channel_id=1, source_target_pairs={{0,1},{1,2},{2,3},{4,5},{5,6},{6,7},{8,9},{9,10},{10,11},{12,13},{... | collective-permute-start | bytes 49160 | tf_op jit(solution)/shard_map/ppermute | solution.py:18
  72.8 3.0 %collective-permute-start.10 = (bf16[1,64,1,128]{1,3,2,0:T(8,128)(2,1)S(1)}, bf16[1,64,1,128]{1,3,2,0:T(8,128)(2,1)S(1)}, u32[]{:S(2)}, u32[]{:S(2)}) collective-permute-start(bf16[1,64,1,128]{1,3,2,0:T(8,128)(2,1)S(1)} %get-tuple-element.164), channel_id=1, source_target_pairs={{0,1},{1,2},{2,3},{4,5},{5,6},{6,7},{8,9},{9,10},{10,11},{12,13},{... | collective-permute-start | bytes 49160 | tf_op jit(solution)/shard_map/ppermute | solution.py:18
  77.8 2.0 collective-permute-done.11
  83.6 4.5 %collective-permute-start.16 = (bf16[1,128,1,128]{1,3,2,0:T(8,128)(2,1)S(1)}, bf16[1,128,1,128]{1,3,2,0:T(8,128)(2,1)S(1)}, u32[]{:S(2)}, u32[]{:S(2)}) collective-permute-start(bf16[1,128,1,128]{1,3,2,0:T(8,128)(2,1)S(1)} %get-tuple-element.168), channel_id=1, source_target_pairs={{0,1},{1,2},{2,3},{4,5},{5,6},{6,7},{8,9},{9,10},{10,11},{12,13},{... | collective-permute-start | bytes 98312 | tf_op jit(solution)/shard_map/ppermute | solution.py:18
  89.5 3.0 %collective-permute-start.12 = (bf16[1,128,1,128]{1,3,2,0:T(8,128)(2,1)S(1)}, bf16[1,128,1,128]{1,3,2,0:T(8,128)(2,1)S(1)}, u32[]{:S(2)}, u32[]{:S(2)}) collective-permute-start(bf16[1,128,1,128]{1,3,2,0:T(8,128)(2,1)S(1)} %get-tuple-element.160), channel_id=1, source_target_pairs={{0,1},{1,2},{2,3},{4,5},{5,6},{6,7},{8,9},{9,10},{10,11},{12,13},{... | collective-permute-start | bytes 98312 | tf_op jit(solution)/shard_map/ppermute | solution.py:18
  100.4 4.7 %collective-permute-start.18 = (bf16[1,128,1,128]{1,3,2,0:T(8,128)(2,1)S(1)}, bf16[1,128,1,128]{1,3,2,0:T(8,128)(2,1)S(1)}, u32[]{:S(2)}, u32[]{:S(2)}) collective-permute-start(bf16[1,128,1,128]{1,3,2,0:T(8,128)(2,1)S(1)} %get-tuple-element.156), channel_id=1, source_target_pairs={{0,1},{1,2},{2,3},{4,5},{5,6},{6,7},{8,9},{9,10},{10,11},{12,13},{... | collective-permute-start | bytes 98312 | tf_op jit(solution)/shard_map/ppermute | solution.py:18
  106.4 1.8 collective-permute-done.19
  110.4 4.1 %collective-permute-start.20 = (bf16[1,128,1,128]{1,3,2,0:T(8,128)(2,1)S(1)}, bf16[1,128,1,128]{1,3,2,0:T(8,128)(2,1)S(1)}, u32[]{:S(2)}, u32[]{:S(2)}) collective-permute-start(bf16[1,128,1,128]{1,3,2,0:T(8,128)(2,1)S(1)} %get-tuple-element.152), channel_id=1, source_target_pairs={{0,1},{1,2},{2,3},{4,5},{5,6},{6,7},{8,9},{9,10},{10,11},{12,13},{... | collective-permute-start | bytes 98312 | tf_op jit(solution)/shard_map/ppermute | solution.py:18
  116.1 1.7 multiply_reduce_fusion
  124.0 2.0 fusion.35
  126.7 3.6 %collective-permute-start.22 = (bf16[1,64,1,256]{3,2,1,0:T(2,128)(2,1)}, bf16[1,64,1,256]{3,2,1,0:T(2,128)(2,1)}, u32[]{:S(2)}, u32[]{:S(2)}) collective-permute-start(bf16[1,64,1,256]{3,2,1,0:T(2,128)(2,1)} %get-tuple-element.104), channel_id=1, source_target_pairs={{0,1},{1,2},{2,3},{4,5},{5,6},{6,7},{8,9},{9,10},{10,11},{12,13},{... | collective-permute-start | bytes 98312 | tf_op jit(solution)/shard_map/ppermute | solution.py:18
  141.2 3.3 %collective-permute-start.24 = (bf16[1,64,1,256]{3,2,1,0:T(2,128)(2,1)S(1)}, bf16[1,64,1,256]{3,2,1,0:T(2,128)(2,1)S(1)}, u32[]{:S(2)}, u32[]{:S(2)}) collective-permute-start(bf16[1,64,1,256]{3,2,1,0:T(2,128)(2,1)S(1)} %get-tuple-element.100), channel_id=1, source_target_pairs={{0,1},{1,2},{2,3},{4,5},{5,6},{6,7},{8,9},{9,10},{10,11},{12,13},{... | collective-permute-start | bytes 98312 | tf_op jit(solution)/shard_map/ppermute | solution.py:18
  146.0 2.8 %collective-permute-done.25 = bf16[1,64,1,256]{3,2,1,0:T(2,128)(2,1)S(1)} collective-permute-done((bf16[1,64,1,256]{3,2,1,0:T(2,128)(2,1)S(1)}, bf16[1,64,1,256]{3,2,1,0:T(2,128)(2,1)S(1)}, u32[]{:S(2)}, u32[]{:S(2)}) %collective-permute-start.25) | collective-permute-done | bytes 32800 | tf_op jit(solution)/shard_map/ppermute | solution.py:19
  151.5 4.8 %collective-permute-start.26 = (bf16[1,3,1,256]{3,1,2,0:T(4,128)(2,1)S(1)}, bf16[1,3,1,256]{3,1,2,0:T(4,128)(2,1)S(1)}, u32[]{:S(2)}, u32[]{:S(2)}) collective-permute-start(bf16[1,3,1,256]{3,1,2,0:T(4,128)(2,1)S(1)} %get-tuple-element.194), channel_id=1, source_target_pairs={{0,1},{1,2},{2,3},{4,5},{5,6},{6,7},{8,9},{9,10},{10,11},{12,13},{... | collective-permute-start | bytes 4616 | tf_op jit(solution)/shard_map/ppermute | solution.py:18
  156.4 1.6 collective-permute-start.27
  166.7 41.5 %all-reduce.17 = (f32[]{:T(128)}, f32[3,128,3,3]{1,3,2,0:T(4,128)}, f32[3]{0:T(128)}) all-reduce(f32[]{:T(128)S(6)} %add.1136, f32[3,128,3,3]{1,3,2,0:T(4,128)S(1)} %bitcast.1222, f32[3]{0:T(128)S(1)} %get-tuple-element.57), channel_id=1, replica_groups=mesh['clip'=8,'row'=4] {'clip','row'}, use_global_device_ids=true, to_apply=%region_8.9 | all-reduce | flops 3460 | bytes 27680 | tf_op jit(solution)/shard_map/psum | solution.py:210
  (418 shorter events, 87.7 us)
Async XLA Ops:
  3.4 12.2 %collective-permute-start = (f32[1,3,256]{2,1,0:T(4,128)S(1)}, f32[1,3,256]{2,1,0:T(4,128)S(1)}, u32[]{:S(2)}, u32[]{:S(2)}) collective-permute-start(f32[1,3,256]{2,1,0:T(4,128)S(1)} %fusion.18), channel_id=1, source_target_pairs={{0,1},{1,2},{2,3},{4,5},{5,6},{6,7},{8,9},{9,10},{10,11},{12,13},{... | collective-permute-start | bytes 9224 | tf_op jit(solution)/shard_map/ppermute | solution.py:27
  6.4 9.2 %collective-permute-start.1 = (f32[1,3,256]{2,1,0:T(4,128)S(1)}, f32[1,3,256]{2,1,0:T(4,128)S(1)}, u32[]{:S(2)}, u32[]{:S(2)}) collective-permute-start(f32[1,3,256]{2,1,0:T(4,128)S(1)} %fusion.17), channel_id=1, source_target_pairs={{1,0},{2,1},{3,2},{5,4},{6,5},{7,6},{9,8},{10,9},{11,10},{13,12},{... | collective-permute-start | bytes 9224 | tf_op jit(solution)/shard_map/ppermute | solution.py:27
  15.8 12.1 %collective-permute-start.2 = (bf16[1,3,1,256]{3,1,2,0:T(4,128)(2,1)S(1)}, bf16[1,3,1,256]{3,1,2,0:T(4,128)(2,1)S(1)}, u32[]{:S(2)}, u32[]{:S(2)}) collective-permute-start(bf16[1,3,1,256]{3,1,2,0:T(4,128)(2,1)S(1)} %get-tuple-element.202), channel_id=1, source_target_pairs={{0,1},{1,2},{2,3},{4,5},{5,6},{6,7},{8,9},{9,10},{10,11},{12,13},{... | collective-permute-start | bytes 4616 | tf_op jit(solution)/shard_map/ppermute | solution.py:18
  20.9 6.9 %collective-permute-start.3 = (bf16[1,3,1,256]{3,1,2,0:T(4,128)(2,1)S(1)}, bf16[1,3,1,256]{3,1,2,0:T(4,128)(2,1)S(1)}, u32[]{:S(2)}, u32[]{:S(2)}) collective-permute-start(bf16[1,3,1,256]{3,1,2,0:T(4,128)(2,1)S(1)} %get-tuple-element.203), channel_id=1, source_target_pairs={{1,0},{2,1},{3,2},{5,4},{6,5},{7,6},{9,8},{10,9},{11,10},{13,12},{... | collective-permute-start | bytes 4616 | tf_op jit(solution)/shard_map/ppermute | solution.py:19
  22.2 8.5 %collective-permute-start.6 = (bf16[1,3,1,256]{3,1,2,0:T(4,128)(2,1)S(1)}, bf16[1,3,1,256]{3,1,2,0:T(4,128)(2,1)S(1)}, u32[]{:S(2)}, u32[]{:S(2)}) collective-permute-start(bf16[1,3,1,256]{3,1,2,0:T(4,128)(2,1)S(1)} %get-tuple-element.198), channel_id=1, source_target_pairs={{0,1},{1,2},{2,3},{4,5},{5,6},{6,7},{8,9},{9,10},{10,11},{12,13},{... | collective-permute-start | bytes 4616 | tf_op jit(solution)/shard_map/ppermute | solution.py:18
  26.5 4.3 %collective-permute-start.7 = (bf16[1,3,1,256]{3,1,2,0:T(4,128)(2,1)S(1)}, bf16[1,3,1,256]{3,1,2,0:T(4,128)(2,1)S(1)}, u32[]{:S(2)}, u32[]{:S(2)}) collective-permute-start(bf16[1,3,1,256]{3,1,2,0:T(4,128)(2,1)S(1)} %get-tuple-element.199), channel_id=1, source_target_pairs={{1,0},{2,1},{3,2},{5,4},{6,5},{7,6},{9,8},{10,9},{11,10},{13,12},{... | collective-permute-start | bytes 4616 | tf_op jit(solution)/shard_map/ppermute | solution.py:19
  34.3 11.5 %collective-permute-start.8 = (bf16[1,64,1,256]{3,2,1,0:T(2,128)(2,1)S(1)}, bf16[1,64,1,256]{3,2,1,0:T(2,128)(2,1)S(1)}, u32[]{:S(2)}, u32[]{:S(2)}) collective-permute-start(bf16[1,64,1,256]{3,2,1,0:T(2,128)(2,1)S(1)} %get-tuple-element.108), channel_id=1, source_target_pairs={{0,1},{1,2},{2,3},{4,5},{5,6},{6,7},{8,9},{9,10},{10,11},{12,13},{... | collective-permute-start | bytes 98312 | tf_op jit(solution)/shard_map/ppermute | solution.py:18
  38.5 7.2 %collective-permute-start.9 = (bf16[1,64,1,256]{3,2,1,0:T(2,128)(2,1)S(1)}, bf16[1,64,1,256]{3,2,1,0:T(2,128)(2,1)S(1)}, u32[]{:S(2)}, u32[]{:S(2)}) collective-permute-start(bf16[1,64,1,256]{3,2,1,0:T(2,128)(2,1)S(1)} %get-tuple-element.109), channel_id=1, source_target_pairs={{1,0},{2,1},{3,2},{5,4},{6,5},{7,6},{9,8},{10,9},{11,10},{13,12},{... | collective-permute-start | bytes 98312 | tf_op jit(solution)/shard_map/ppermute | solution.py:19
  40.1 6.1 %collective-permute-start.4 = (bf16[1,64,1,256]{3,2,1,0:T(2,128)(2,1)S(1)}, bf16[1,64,1,256]{3,2,1,0:T(2,128)(2,1)S(1)}, u32[]{:S(2)}, u32[]{:S(2)}) collective-permute-start(bf16[1,64,1,256]{3,2,1,0:T(2,128)(2,1)S(1)} %get-tuple-element.112), channel_id=1, source_target_pairs={{0,1},{1,2},{2,3},{4,5},{5,6},{6,7},{8,9},{9,10},{10,11},{12,13},{... | collective-permute-start | bytes 98312 | tf_op jit(solution)/shard_map/ppermute | solution.py:18
  44.3 4.4 %collective-permute-start.5 = (bf16[1,64,1,256]{3,2,1,0:T(2,128)(2,1)S(1)}, bf16[1,64,1,256]{3,2,1,0:T(2,128)(2,1)S(1)}, u32[]{:S(2)}, u32[]{:S(2)}) collective-permute-start(bf16[1,64,1,256]{3,2,1,0:T(2,128)(2,1)S(1)} %get-tuple-element.113), channel_id=1, source_target_pairs={{1,0},{2,1},{3,2},{5,4},{6,5},{7,6},{9,8},{10,9},{11,10},{13,12},{... | collective-permute-start | bytes 98312 | tf_op jit(solution)/shard_map/ppermute | solution.py:19
  66.5 10.7 %collective-permute-start.14 = (bf16[1,64,1,128]{1,3,2,0:T(8,128)(2,1)S(1)}, bf16[1,64,1,128]{1,3,2,0:T(8,128)(2,1)S(1)}, u32[]{:S(2)}, u32[]{:S(2)}) collective-permute-start(bf16[1,64,1,128]{1,3,2,0:T(8,128)(2,1)S(1)} %get-tuple-element.172), channel_id=1, source_target_pairs={{0,1},{1,2},{2,3},{4,5},{5,6},{6,7},{8,9},{9,10},{10,11},{12,13},{... | collective-permute-start | bytes 49160 | tf_op jit(solution)/shard_map/ppermute | solution.py:18
  71.4 5.8 %collective-permute-start.15 = (bf16[1,64,1,128]{1,3,2,0:T(8,128)(2,1)S(1)}, bf16[1,64,1,128]{1,3,2,0:T(8,128)(2,1)S(1)}, u32[]{:S(2)}, u32[]{:S(2)}) collective-permute-start(bf16[1,64,1,128]{1,3,2,0:T(8,128)(2,1)S(1)} %get-tuple-element.173), channel_id=1, source_target_pairs={{1,0},{2,1},{3,2},{5,4},{6,5},{7,6},{9,8},{10,9},{11,10},{13,12},{... | collective-permute-start | bytes 49160 | tf_op jit(solution)/shard_map/ppermute | solution.py:19
  72.8 4.9 %collective-permute-start.10 = (bf16[1,64,1,128]{1,3,2,0:T(8,128)(2,1)S(1)}, bf16[1,64,1,128]{1,3,2,0:T(8,128)(2,1)S(1)}, u32[]{:S(2)}, u32[]{:S(2)}) collective-permute-start(bf16[1,64,1,128]{1,3,2,0:T(8,128)(2,1)S(1)} %get-tuple-element.164), channel_id=1, source_target_pairs={{0,1},{1,2},{2,3},{4,5},{5,6},{6,7},{8,9},{9,10},{10,11},{12,13},{... | collective-permute-start | bytes 49160 | tf_op jit(solution)/shard_map/ppermute | solution.py:18
  83.6 10.2 %collective-permute-start.16 = (bf16[1,128,1,128]{1,3,2,0:T(8,128)(2,1)S(1)}, bf16[1,128,1,128]{1,3,2,0:T(8,128)(2,1)S(1)}, u32[]{:S(2)}, u32[]{:S(2)}) collective-permute-start(bf16[1,128,1,128]{1,3,2,0:T(8,128)(2,1)S(1)} %get-tuple-element.168), channel_id=1, source_target_pairs={{0,1},{1,2},{2,3},{4,5},{5,6},{6,7},{8,9},{9,10},{10,11},{12,13},{... | collective-permute-start | bytes 98312 | tf_op jit(solution)/shard_map/ppermute | solution.py:18
  88.1 5.7 %collective-permute-start.17 = (bf16[1,128,1,128]{1,3,2,0:T(8,128)(2,1)S(1)}, bf16[1,128,1,128]{1,3,2,0:T(8,128)(2,1)S(1)}, u32[]{:S(2)}, u32[]{:S(2)}) collective-permute-start(bf16[1,128,1,128]{1,3,2,0:T(8,128)(2,1)S(1)} %get-tuple-element.169), channel_id=1, source_target_pairs={{1,0},{2,1},{3,2},{5,4},{6,5},{7,6},{9,8},{10,9},{11,10},{13,12},{... | collective-permute-start | bytes 98312 | tf_op jit(solution)/shard_map/ppermute | solution.py:19
  89.5 5.7 %collective-permute-start.12 = (bf16[1,128,1,128]{1,3,2,0:T(8,128)(2,1)S(1)}, bf16[1,128,1,128]{1,3,2,0:T(8,128)(2,1)S(1)}, u32[]{:S(2)}, u32[]{:S(2)}) collective-permute-start(bf16[1,128,1,128]{1,3,2,0:T(8,128)(2,1)S(1)} %get-tuple-element.160), channel_id=1, source_target_pairs={{0,1},{1,2},{2,3},{4,5},{5,6},{6,7},{8,9},{9,10},{10,11},{12,13},{... | collective-permute-start | bytes 98312 | tf_op jit(solution)/shard_map/ppermute | solution.py:18
  100.4 6.0 %collective-permute-start.18 = (bf16[1,128,1,128]{1,3,2,0:T(8,128)(2,1)S(1)}, bf16[1,128,1,128]{1,3,2,0:T(8,128)(2,1)S(1)}, u32[]{:S(2)}, u32[]{:S(2)}) collective-permute-start(bf16[1,128,1,128]{1,3,2,0:T(8,128)(2,1)S(1)} %get-tuple-element.156), channel_id=1, source_target_pairs={{0,1},{1,2},{2,3},{4,5},{5,6},{6,7},{8,9},{9,10},{10,11},{12,13},{... | collective-permute-start | bytes 98312 | tf_op jit(solution)/shard_map/ppermute | solution.py:18
  110.4 9.3 %collective-permute-start.20 = (bf16[1,128,1,128]{1,3,2,0:T(8,128)(2,1)S(1)}, bf16[1,128,1,128]{1,3,2,0:T(8,128)(2,1)S(1)}, u32[]{:S(2)}, u32[]{:S(2)}) collective-permute-start(bf16[1,128,1,128]{1,3,2,0:T(8,128)(2,1)S(1)} %get-tuple-element.152), channel_id=1, source_target_pairs={{0,1},{1,2},{2,3},{4,5},{5,6},{6,7},{8,9},{9,10},{10,11},{12,13},{... | collective-permute-start | bytes 98312 | tf_op jit(solution)/shard_map/ppermute | solution.py:18
  114.5 5.2 %collective-permute-start.21 = (bf16[1,128,1,128]{1,3,2,0:T(8,128)(2,1)S(1)}, bf16[1,128,1,128]{1,3,2,0:T(8,128)(2,1)S(1)}, u32[]{:S(2)}, u32[]{:S(2)}) collective-permute-start(bf16[1,128,1,128]{1,3,2,0:T(8,128)(2,1)S(1)} %get-tuple-element.153), channel_id=1, source_target_pairs={{1,0},{2,1},{3,2},{5,4},{6,5},{7,6},{9,8},{10,9},{11,10},{13,12},{... | collective-permute-start | bytes 98312 | tf_op jit(solution)/shard_map/ppermute | solution.py:19
  126.7 7.8 %collective-permute-start.22 = (bf16[1,64,1,256]{3,2,1,0:T(2,128)(2,1)}, bf16[1,64,1,256]{3,2,1,0:T(2,128)(2,1)}, u32[]{:S(2)}, u32[]{:S(2)}) collective-permute-start(bf16[1,64,1,256]{3,2,1,0:T(2,128)(2,1)} %get-tuple-element.104), channel_id=1, source_target_pairs={{0,1},{1,2},{2,3},{4,5},{5,6},{6,7},{8,9},{9,10},{10,11},{12,13},{... | collective-permute-start | bytes 98312 | tf_op jit(solution)/shard_map/ppermute | solution.py:18
  130.4 5.0 %collective-permute-start.23 = (bf16[1,64,1,256]{3,2,1,0:T(2,128)(2,1)}, bf16[1,64,1,256]{3,2,1,0:T(2,128)(2,1)S(1)}, u32[]{:S(2)}, u32[]{:S(2)}) collective-permute-start(bf16[1,64,1,256]{3,2,1,0:T(2,128)(2,1)} %get-tuple-element.105), channel_id=1, source_target_pairs={{1,0},{2,1},{3,2},{5,4},{6,5},{7,6},{9,8},{10,9},{11,10},{13,12},{... | collective-permute-start | bytes 98312 | tf_op jit(solution)/shard_map/ppermute | solution.py:19
  141.2 4.8 %collective-permute-start.24 = (bf16[1,64,1,256]{3,2,1,0:T(2,128)(2,1)S(1)}, bf16[1,64,1,256]{3,2,1,0:T(2,128)(2,1)S(1)}, u32[]{:S(2)}, u32[]{:S(2)}) collective-permute-start(bf16[1,64,1,256]{3,2,1,0:T(2,128)(2,1)S(1)} %get-tuple-element.100), channel_id=1, source_target_pairs={{0,1},{1,2},{2,3},{4,5},{5,6},{6,7},{8,9},{9,10},{10,11},{12,13},{... | collective-permute-start | bytes 98312 | tf_op jit(solution)/shard_map/ppermute | solution.py:18
  144.5 4.2 %collective-permute-start.25 = (bf16[1,64,1,256]{3,2,1,0:T(2,128)(2,1)S(1)}, bf16[1,64,1,256]{3,2,1,0:T(2,128)(2,1)S(1)}, u32[]{:S(2)}, u32[]{:S(2)}) collective-permute-start(bf16[1,64,1,256]{3,2,1,0:T(2,128)(2,1)S(1)} %get-tuple-element.101), channel_id=1, source_target_pairs={{1,0},{2,1},{3,2},{5,4},{6,5},{7,6},{9,8},{10,9},{11,10},{13,12},{... | collective-permute-start | bytes 98312 | tf_op jit(solution)/shard_map/ppermute | solution.py:19
  151.5 7.7 %collective-permute-start.26 = (bf16[1,3,1,256]{3,1,2,0:T(4,128)(2,1)S(1)}, bf16[1,3,1,256]{3,1,2,0:T(4,128)(2,1)S(1)}, u32[]{:S(2)}, u32[]{:S(2)}) collective-permute-start(bf16[1,3,1,256]{3,1,2,0:T(4,128)(2,1)S(1)} %get-tuple-element.194), channel_id=1, source_target_pairs={{0,1},{1,2},{2,3},{4,5},{5,6},{6,7},{8,9},{9,10},{10,11},{12,13},{... | collective-permute-start | bytes 4616 | tf_op jit(solution)/shard_map/ppermute | solution.py:18
  (43 other events, 118.7 us)
where the time goes:
time: 210 us; the launch traced here: 208 us
  starting transfers between devices  75.1 us (36%)
  blocking collectives  41.5 us (20%)
  matrix products  32.7 us (16%)
  local copies, waits for them, and re-layouts  32.1 us (15%)
  other arithmetic  11.8 us (6%)
  waiting for transfers between devices  10.5 us (5%)
  between operations  4.34 us (2%)
    ppermute x13, starting transfers between devices, padded_2(): before = lax.ppermute(last, axis, up)  53.9 us
    psum x1, blocking collectives, local(): lax.psum((part_one + part_two, weight_grad, bias_grad), ('clip', 'row'))  41.5 us
    dot_general x126, matrix products, conv_valid(): jnp.dot(weight[:, :, row_shift, col_shift], piece.reshape(channels, row_c...  29.1 us
    ppermute x13, starting transfers between devices, padded_2(): after = lax.ppermute(leading, axis, down)  17.6 us
    unnamed x129, local copies, waits for them, and re-layouts  11.2 us
    ppermute x13, waiting for transfers between devices, padded_2(): after = lax.ppermute(leading, axis, down)  10.5 us
  transfers between devices with their start and end apart: 28, of which 7 were waited for; matrix products, arithmetic and copies ran while one was open for 10% of the time, Pallas kernels for 0%

commit v1 on v0

--- a/solution.py
+++ b/solution.py
@@ -208,7 +208,7 @@
     weight_grad = grad_from_output(features, grad_pad)
     bias_grad = jnp.sum(grad_dec.astype(jnp.float32), (0, 2, 3))
     loss, weight_total, bias_total = lax.psum(
-        (part_one + part_two, weight_grad, bias_grad), ("clip", "row")
+        lax.psum((part_one + part_two, weight_grad, bias_grad), "row"), "clip"
     )
     return (loss, feature_grad, weight_total, bias_total)
 

time: 210 us -> 219 us (1.043)
  blocking collectives: 41.5 us -> 51.1 us
    psum x1 -> x2, blocking collectives: 41.5 us -> 51.1 us  [the longest x1 38.6 us: local(): lax.psum(lax.psum((part_one + part_two, weight_grad, bias_grad), 'row'),...]
  transfers between devices with their start and end apart: 28 -> 28, of which waited for: 7 -> 7; matrix products, arithmetic and copies ran while one was open for 10% -> 9% of each run, Pallas kernels for 0% -> 0%
where the time goes in v1:
time: 219 us; the launch traced here: 218 us
  starting transfers between devices  75.1 us (34%)
  blocking collectives  51.1 us (23%)
  matrix products  32.8 us (15%)
  local copies, waits for them, and re-layouts  32.1 us (15%)
  other arithmetic  11.9 us (5%)
  waiting for transfers between devices  10.5 us (5%)
  between operations  4.42 us (2%)
    ppermute x13, starting transfers between devices, padded_2(): before = lax.ppermute(last, axis, up)  53.9 us
    psum x1, blocking collectives, local(): lax.psum(lax.psum((part_one + part_two, weight_grad, bias_grad), 'row'),...  38.6 us
    dot_general x126, matrix products, conv_valid(): jnp.dot(weight[:, :, row_shift, col_shift], piece.reshape(channels, row_c...  29.1 us
    ppermute x13, starting transfers between devices, padded_2(): after = lax.ppermute(leading, axis, down)  17.6 us
    psum x1, blocking collectives, local(): lax.psum((part_one + part_two, weight_grad, bias_grad), 'row')  12.5 us
    unnamed x129, local copies, waits for them, and re-layouts  11.2 us
    ppermute x13, waiting for transfers between devices, padded_2(): after = lax.ppermute(leading, axis, down)  10.4 us
  transfers between devices with their start and end apart: 28, of which 7 were waited for; matrix products, arithmetic and copies ran while one was open for 9% of the time, Pallas kernels for 0%

profile of v1, /device:TPU:0, one launch (start us, length us, event | category | flops | bytes accessed | tf_op | source)
XLA Modules:
  0.0 217.9 jit_solution(12393790961910581182)
XLA Ops:
  3.4 2.4 %collective-permute-start = (f32[1,3,256]{2,1,0:T(4,128)S(1)}, f32[1,3,256]{2,1,0:T(4,128)S(1)}, u32[]{:S(2)}, u32[]{:S(2)}) collective-permute-start(f32[1,3,256]{2,1,0:T(4,128)S(1)} %fusion.18), channel_id=1, source_target_pairs={{0,1},{1,2},{2,3},{4,5},{5,6},{6,7},{8,9},{9,10},{10,11},{12,13},{... | collective-permute-start | bytes 9224 | tf_op jit(solution)/shard_map/ppermute | solution.py:27
  15.7 5.2 %collective-permute-start.2 = (bf16[1,3,1,256]{3,1,2,0:T(4,128)(2,1)S(1)}, bf16[1,3,1,256]{3,1,2,0:T(4,128)(2,1)S(1)}, u32[]{:S(2)}, u32[]{:S(2)}) collective-permute-start(bf16[1,3,1,256]{3,1,2,0:T(4,128)(2,1)S(1)} %get-tuple-element.205), channel_id=1, source_target_pairs={{0,1},{1,2},{2,3},{4,5},{5,6},{6,7},{8,9},{9,10},{10,11},{12,13},{... | collective-permute-start | bytes 4616 | tf_op jit(solution)/shard_map/ppermute | solution.py:18
  22.2 4.3 %collective-permute-start.6 = (bf16[1,3,1,256]{3,1,2,0:T(4,128)(2,1)S(1)}, bf16[1,3,1,256]{3,1,2,0:T(4,128)(2,1)S(1)}, u32[]{:S(2)}, u32[]{:S(2)}) collective-permute-start(bf16[1,3,1,256]{3,1,2,0:T(4,128)(2,1)S(1)} %get-tuple-element.201), channel_id=1, source_target_pairs={{0,1},{1,2},{2,3},{4,5},{5,6},{6,7},{8,9},{9,10},{10,11},{12,13},{... | collective-permute-start | bytes 4616 | tf_op jit(solution)/shard_map/ppermute | solution.py:18
  34.2 4.3 %collective-permute-start.8 = (bf16[1,64,1,256]{3,2,1,0:T(2,128)(2,1)S(1)}, bf16[1,64,1,256]{3,2,1,0:T(2,128)(2,1)S(1)}, u32[]{:S(2)}, u32[]{:S(2)}) collective-permute-start(bf16[1,64,1,256]{3,2,1,0:T(2,128)(2,1)S(1)} %get-tuple-element.111), channel_id=1, source_target_pairs={{0,1},{1,2},{2,3},{4,5},{5,6},{6,7},{8,9},{9,10},{10,11},{12,13},{... | collective-permute-start | bytes 98312 | tf_op jit(solution)/shard_map/ppermute | solution.py:18
  40.0 4.2 %collective-permute-start.4 = (bf16[1,64,1,256]{3,2,1,0:T(2,128)(2,1)S(1)}, bf16[1,64,1,256]{3,2,1,0:T(2,128)(2,1)S(1)}, u32[]{:S(2)}, u32[]{:S(2)}) collective-permute-start(bf16[1,64,1,256]{3,2,1,0:T(2,128)(2,1)S(1)} %get-tuple-element.115), channel_id=1, source_target_pairs={{0,1},{1,2},{2,3},{4,5},{5,6},{6,7},{8,9},{9,10},{10,11},{12,13},{... | collective-permute-start | bytes 98312 | tf_op jit(solution)/shard_map/ppermute | solution.py:18
  46.1 2.5 %collective-permute-done.5 = bf16[1,64,1,256]{3,2,1,0:T(2,128)(2,1)S(1)} collective-permute-done((bf16[1,64,1,256]{3,2,1,0:T(2,128)(2,1)S(1)}, bf16[1,64,1,256]{3,2,1,0:T(2,128)(2,1)S(1)}, u32[]{:S(2)}, u32[]{:S(2)}) %collective-permute-start.5) | collective-permute-done | bytes 32800 | tf_op jit(solution)/shard_map/ppermute | solution.py:19
  60.3 2.1 copy.253
  62.5 2.1 multiply_reduce_fusion.2
  66.5 4.8 %collective-permute-start.14 = (bf16[1,64,1,128]{1,3,2,0:T(8,128)(2,1)S(1)}, bf16[1,64,1,128]{1,3,2,0:T(8,128)(2,1)S(1)}, u32[]{:S(2)}, u32[]{:S(2)}) collective-permute-start(bf16[1,64,1,128]{1,3,2,0:T(8,128)(2,1)S(1)} %get-tuple-element.175), channel_id=1, source_target_pairs={{0,1},{1,2},{2,3},{4,5},{5,6},{6,7},{8,9},{9,10},{10,11},{12,13},{... | collective-permute-start | bytes 49160 | tf_op jit(solution)/shard_map/ppermute | solution.py:18
  72.8 3.0 %collective-permute-start.10 = (bf16[1,64,1,128]{1,3,2,0:T(8,128)(2,1)S(1)}, bf16[1,64,1,128]{1,3,2,0:T(8,128)(2,1)S(1)}, u32[]{:S(2)}, u32[]{:S(2)}) collective-permute-start(bf16[1,64,1,128]{1,3,2,0:T(8,128)(2,1)S(1)} %get-tuple-element.167), channel_id=1, source_target_pairs={{0,1},{1,2},{2,3},{4,5},{5,6},{6,7},{8,9},{9,10},{10,11},{12,13},{... | collective-permute-start | bytes 49160 | tf_op jit(solution)/shard_map/ppermute | solution.py:18
  77.8 2.0 collective-permute-done.11
  83.6 4.5 %collective-permute-start.16 = (bf16[1,128,1,128]{1,3,2,0:T(8,128)(2,1)S(1)}, bf16[1,128,1,128]{1,3,2,0:T(8,128)(2,1)S(1)}, u32[]{:S(2)}, u32[]{:S(2)}) collective-permute-start(bf16[1,128,1,128]{1,3,2,0:T(8,128)(2,1)S(1)} %get-tuple-element.171), channel_id=1, source_target_pairs={{0,1},{1,2},{2,3},{4,5},{5,6},{6,7},{8,9},{9,10},{10,11},{12,13},{... | collective-permute-start | bytes 98312 | tf_op jit(solution)/shard_map/ppermute | solution.py:18
  89.5 3.0 %collective-permute-start.12 = (bf16[1,128,1,128]{1,3,2,0:T(8,128)(2,1)S(1)}, bf16[1,128,1,128]{1,3,2,0:T(8,128)(2,1)S(1)}, u32[]{:S(2)}, u32[]{:S(2)}) collective-permute-start(bf16[1,128,1,128]{1,3,2,0:T(8,128)(2,1)S(1)} %get-tuple-element.163), channel_id=1, source_target_pairs={{0,1},{1,2},{2,3},{4,5},{5,6},{6,7},{8,9},{9,10},{10,11},{12,13},{... | collective-permute-start | bytes 98312 | tf_op jit(solution)/shard_map/ppermute | solution.py:18
  100.4 4.7 %collective-permute-start.18 = (bf16[1,128,1,128]{1,3,2,0:T(8,128)(2,1)S(1)}, bf16[1,128,1,128]{1,3,2,0:T(8,128)(2,1)S(1)}, u32[]{:S(2)}, u32[]{:S(2)}) collective-permute-start(bf16[1,128,1,128]{1,3,2,0:T(8,128)(2,1)S(1)} %get-tuple-element.159), channel_id=1, source_target_pairs={{0,1},{1,2},{2,3},{4,5},{5,6},{6,7},{8,9},{9,10},{10,11},{12,13},{... | collective-permute-start | bytes 98312 | tf_op jit(solution)/shard_map/ppermute | solution.py:18
  106.4 1.8 collective-permute-done.19
  110.5 4.0 %collective-permute-start.20 = (bf16[1,128,1,128]{1,3,2,0:T(8,128)(2,1)S(1)}, bf16[1,128,1,128]{1,3,2,0:T(8,128)(2,1)S(1)}, u32[]{:S(2)}, u32[]{:S(2)}) collective-permute-start(bf16[1,128,1,128]{1,3,2,0:T(8,128)(2,1)S(1)} %get-tuple-element.155), channel_id=1, source_target_pairs={{0,1},{1,2},{2,3},{4,5},{5,6},{6,7},{8,9},{9,10},{10,11},{12,13},{... | collective-permute-start | bytes 98312 | tf_op jit(solution)/shard_map/ppermute | solution.py:18
  116.1 1.7 multiply_reduce_fusion
  124.1 2.0 fusion.35
  126.8 3.7 %collective-permute-start.22 = (bf16[1,64,1,256]{3,2,1,0:T(2,128)(2,1)}, bf16[1,64,1,256]{3,2,1,0:T(2,128)(2,1)}, u32[]{:S(2)}, u32[]{:S(2)}) collective-permute-start(bf16[1,64,1,256]{3,2,1,0:T(2,128)(2,1)} %get-tuple-element.107), channel_id=1, source_target_pairs={{0,1},{1,2},{2,3},{4,5},{5,6},{6,7},{8,9},{9,10},{10,11},{12,13},{... | collective-permute-start | bytes 98312 | tf_op jit(solution)/shard_map/ppermute | solution.py:18
  141.2 3.3 %collective-permute-start.24 = (bf16[1,64,1,256]{3,2,1,0:T(2,128)(2,1)S(1)}, bf16[1,64,1,256]{3,2,1,0:T(2,128)(2,1)S(1)}, u32[]{:S(2)}, u32[]{:S(2)}) collective-permute-start(bf16[1,64,1,256]{3,2,1,0:T(2,128)(2,1)S(1)} %get-tuple-element.103), channel_id=1, source_target_pairs={{0,1},{1,2},{2,3},{4,5},{5,6},{6,7},{8,9},{9,10},{10,11},{12,13},{... | collective-permute-start | bytes 98312 | tf_op jit(solution)/shard_map/ppermute | solution.py:18
  146.0 2.8 %collective-permute-done.25 = bf16[1,64,1,256]{3,2,1,0:T(2,128)(2,1)S(1)} collective-permute-done((bf16[1,64,1,256]{3,2,1,0:T(2,128)(2,1)S(1)}, bf16[1,64,1,256]{3,2,1,0:T(2,128)(2,1)S(1)}, u32[]{:S(2)}, u32[]{:S(2)}) %collective-permute-start.25) | collective-permute-done | bytes 32800 | tf_op jit(solution)/shard_map/ppermute | solution.py:19
  151.6 4.8 %collective-permute-start.26 = (bf16[1,3,1,256]{3,1,2,0:T(4,128)(2,1)S(1)}, bf16[1,3,1,256]{3,1,2,0:T(4,128)(2,1)S(1)}, u32[]{:S(2)}, u32[]{:S(2)}) collective-permute-start(bf16[1,3,1,256]{3,1,2,0:T(4,128)(2,1)S(1)} %get-tuple-element.197), channel_id=1, source_target_pairs={{0,1},{1,2},{2,3},{4,5},{5,6},{6,7},{8,9},{9,10},{10,11},{12,13},{... | collective-permute-start | bytes 4616 | tf_op jit(solution)/shard_map/ppermute | solution.py:18
  166.8 12.5 %all-reduce.18 = (f32[]{:T(128)}, f32[3,128,3,3]{1,3,2,0:T(4,128)S(1)}, f32[3]{0:T(128)S(1)}) all-reduce(f32[]{:T(128)S(6)} %add.1142, f32[3,128,3,3]{1,3,2,0:T(4,128)S(1)} %bitcast.1222, f32[3]{0:T(128)S(1)} %get-tuple-element.60), channel_id=1, replica_groups=mesh['clip'=8,'row'=4] {'row'}, use_global_device_ids=true, to_apply=%region_8.9 | all-reduce | flops 3460 | bytes 27680 | tf_op jit(solution)/shard_map/psum | solution.py:211
  179.3 38.6 %all-reduce.17 = (f32[]{:T(128)}, f32[3,128,3,3]{1,3,2,0:T(4,128)}, f32[3]{0:T(128)}) all-reduce(f32[]{:T(128)} %get-tuple-element.57, f32[3,128,3,3]{1,3,2,0:T(4,128)S(1)} %get-tuple-element.58, f32[3]{0:T(128)S(1)} %get-tuple-element.59), channel_id=1, replica_groups=mesh['clip'=8,'row'=4] {'clip'}, use_global_device_ids=true, to_apply=%region_9.10 | all-reduce | flops 3460 | bytes 27680 | tf_op jit(solution)/shard_map/psum | solution.py:210
  (419 shorter events, 89.2 us)
Async XLA Ops:
  3.4 12.1 %collective-permute-start = (f32[1,3,256]{2,1,0:T(4,128)S(1)}, f32[1,3,256]{2,1,0:T(4,128)S(1)}, u32[]{:S(2)}, u32[]{:S(2)}) collective-permute-start(f32[1,3,256]{2,1,0:T(4,128)S(1)} %fusion.18), channel_id=1, source_target_pairs={{0,1},{1,2},{2,3},{4,5},{5,6},{6,7},{8,9},{9,10},{10,11},{12,13},{... | collective-permute-start | bytes 9224 | tf_op jit(solution)/shard_map/ppermute | solution.py:27
  6.4 9.2 %collective-permute-start.1 = (f32[1,3,256]{2,1,0:T(4,128)S(1)}, f32[1,3,256]{2,1,0:T(4,128)S(1)}, u32[]{:S(2)}, u32[]{:S(2)}) collective-permute-start(f32[1,3,256]{2,1,0:T(4,128)S(1)} %fusion.17), channel_id=1, source_target_pairs={{1,0},{2,1},{3,2},{5,4},{6,5},{7,6},{9,8},{10,9},{11,10},{13,12},{... | collective-permute-start | bytes 9224 | tf_op jit(solution)/shard_map/ppermute | solution.py:27
  15.7 12.1 %collective-permute-start.2 = (bf16[1,3,1,256]{3,1,2,0:T(4,128)(2,1)S(1)}, bf16[1,3,1,256]{3,1,2,0:T(4,128)(2,1)S(1)}, u32[]{:S(2)}, u32[]{:S(2)}) collective-permute-start(bf16[1,3,1,256]{3,1,2,0:T(4,128)(2,1)S(1)} %get-tuple-element.205), channel_id=1, source_target_pairs={{0,1},{1,2},{2,3},{4,5},{5,6},{6,7},{8,9},{9,10},{10,11},{12,13},{... | collective-permute-start | bytes 4616 | tf_op jit(solution)/shard_map/ppermute | solution.py:18
  20.9 6.9 %collective-permute-start.3 = (bf16[1,3,1,256]{3,1,2,0:T(4,128)(2,1)S(1)}, bf16[1,3,1,256]{3,1,2,0:T(4,128)(2,1)S(1)}, u32[]{:S(2)}, u32[]{:S(2)}) collective-permute-start(bf16[1,3,1,256]{3,1,2,0:T(4,128)(2,1)S(1)} %get-tuple-element.206), channel_id=1, source_target_pairs={{1,0},{2,1},{3,2},{5,4},{6,5},{7,6},{9,8},{10,9},{11,10},{13,12},{... | collective-permute-start | bytes 4616 | tf_op jit(solution)/shard_map/ppermute | solution.py:19
  22.2 8.5 %collective-permute-start.6 = (bf16[1,3,1,256]{3,1,2,0:T(4,128)(2,1)S(1)}, bf16[1,3,1,256]{3,1,2,0:T(4,128)(2,1)S(1)}, u32[]{:S(2)}, u32[]{:S(2)}) collective-permute-start(bf16[1,3,1,256]{3,1,2,0:T(4,128)(2,1)S(1)} %get-tuple-element.201), channel_id=1, source_target_pairs={{0,1},{1,2},{2,3},{4,5},{5,6},{6,7},{8,9},{9,10},{10,11},{12,13},{... | collective-permute-start | bytes 4616 | tf_op jit(solution)/shard_map/ppermute | solution.py:18
  26.5 4.3 %collective-permute-start.7 = (bf16[1,3,1,256]{3,1,2,0:T(4,128)(2,1)S(1)}, bf16[1,3,1,256]{3,1,2,0:T(4,128)(2,1)S(1)}, u32[]{:S(2)}, u32[]{:S(2)}) collective-permute-start(bf16[1,3,1,256]{3,1,2,0:T(4,128)(2,1)S(1)} %get-tuple-element.202), channel_id=1, source_target_pairs={{1,0},{2,1},{3,2},{5,4},{6,5},{7,6},{9,8},{10,9},{11,10},{13,12},{... | collective-permute-start | bytes 4616 | tf_op jit(solution)/shard_map/ppermute | solution.py:19
  34.2 11.5 %collective-permute-start.8 = (bf16[1,64,1,256]{3,2,1,0:T(2,128)(2,1)S(1)}, bf16[1,64,1,256]{3,2,1,0:T(2,128)(2,1)S(1)}, u32[]{:S(2)}, u32[]{:S(2)}) collective-permute-start(bf16[1,64,1,256]{3,2,1,0:T(2,128)(2,1)S(1)} %get-tuple-element.111), channel_id=1, source_target_pairs={{0,1},{1,2},{2,3},{4,5},{5,6},{6,7},{8,9},{9,10},{10,11},{12,13},{... | collective-permute-start | bytes 98312 | tf_op jit(solution)/shard_map/ppermute | solution.py:18
  38.5 7.2 %collective-permute-start.9 = (bf16[1,64,1,256]{3,2,1,0:T(2,128)(2,1)S(1)}, bf16[1,64,1,256]{3,2,1,0:T(2,128)(2,1)S(1)}, u32[]{:S(2)}, u32[]{:S(2)}) collective-permute-start(bf16[1,64,1,256]{3,2,1,0:T(2,128)(2,1)S(1)} %get-tuple-element.112), channel_id=1, source_target_pairs={{1,0},{2,1},{3,2},{5,4},{6,5},{7,6},{9,8},{10,9},{11,10},{13,12},{... | collective-permute-start | bytes 98312 | tf_op jit(solution)/shard_map/ppermute | solution.py:19
  40.0 6.1 %collective-permute-start.4 = (bf16[1,64,1,256]{3,2,1,0:T(2,128)(2,1)S(1)}, bf16[1,64,1,256]{3,2,1,0:T(2,128)(2,1)S(1)}, u32[]{:S(2)}, u32[]{:S(2)}) collective-permute-start(bf16[1,64,1,256]{3,2,1,0:T(2,128)(2,1)S(1)} %get-tuple-element.115), channel_id=1, source_target_pairs={{0,1},{1,2},{2,3},{4,5},{5,6},{6,7},{8,9},{9,10},{10,11},{12,13},{... | collective-permute-start | bytes 98312 | tf_op jit(solution)/shard_map/ppermute | solution.py:18
  44.2 4.4 %collective-permute-start.5 = (bf16[1,64,1,256]{3,2,1,0:T(2,128)(2,1)S(1)}, bf16[1,64,1,256]{3,2,1,0:T(2,128)(2,1)S(1)}, u32[]{:S(2)}, u32[]{:S(2)}) collective-permute-start(bf16[1,64,1,256]{3,2,1,0:T(2,128)(2,1)S(1)} %get-tuple-element.116), channel_id=1, source_target_pairs={{1,0},{2,1},{3,2},{5,4},{6,5},{7,6},{9,8},{10,9},{11,10},{13,12},{... | collective-permute-start | bytes 98312 | tf_op jit(solution)/shard_map/ppermute | solution.py:19
  66.5 10.7 %collective-permute-start.14 = (bf16[1,64,1,128]{1,3,2,0:T(8,128)(2,1)S(1)}, bf16[1,64,1,128]{1,3,2,0:T(8,128)(2,1)S(1)}, u32[]{:S(2)}, u32[]{:S(2)}) collective-permute-start(bf16[1,64,1,128]{1,3,2,0:T(8,128)(2,1)S(1)} %get-tuple-element.175), channel_id=1, source_target_pairs={{0,1},{1,2},{2,3},{4,5},{5,6},{6,7},{8,9},{9,10},{10,11},{12,13},{... | collective-permute-start | bytes 49160 | tf_op jit(solution)/shard_map/ppermute | solution.py:18
  71.4 5.8 %collective-permute-start.15 = (bf16[1,64,1,128]{1,3,2,0:T(8,128)(2,1)S(1)}, bf16[1,64,1,128]{1,3,2,0:T(8,128)(2,1)S(1)}, u32[]{:S(2)}, u32[]{:S(2)}) collective-permute-start(bf16[1,64,1,128]{1,3,2,0:T(8,128)(2,1)S(1)} %get-tuple-element.176), channel_id=1, source_target_pairs={{1,0},{2,1},{3,2},{5,4},{6,5},{7,6},{9,8},{10,9},{11,10},{13,12},{... | collective-permute-start | bytes 49160 | tf_op jit(solution)/shard_map/ppermute | solution.py:19
  72.8 4.9 %collective-permute-start.10 = (bf16[1,64,1,128]{1,3,2,0:T(8,128)(2,1)S(1)}, bf16[1,64,1,128]{1,3,2,0:T(8,128)(2,1)S(1)}, u32[]{:S(2)}, u32[]{:S(2)}) collective-permute-start(bf16[1,64,1,128]{1,3,2,0:T(8,128)(2,1)S(1)} %get-tuple-element.167), channel_id=1, source_target_pairs={{0,1},{1,2},{2,3},{4,5},{5,6},{6,7},{8,9},{9,10},{10,11},{12,13},{... | collective-permute-start | bytes 49160 | tf_op jit(solution)/shard_map/ppermute | solution.py:18
  83.6 10.2 %collective-permute-start.16 = (bf16[1,128,1,128]{1,3,2,0:T(8,128)(2,1)S(1)}, bf16[1,128,1,128]{1,3,2,0:T(8,128)(2,1)S(1)}, u32[]{:S(2)}, u32[]{:S(2)}) collective-permute-start(bf16[1,128,1,128]{1,3,2,0:T(8,128)(2,1)S(1)} %get-tuple-element.171), channel_id=1, source_target_pairs={{0,1},{1,2},{2,3},{4,5},{5,6},{6,7},{8,9},{9,10},{10,11},{12,13},{... | collective-permute-start | bytes 98312 | tf_op jit(solution)/shard_map/ppermute | solution.py:18
  88.1 5.7 %collective-permute-start.17 = (bf16[1,128,1,128]{1,3,2,0:T(8,128)(2,1)S(1)}, bf16[1,128,1,128]{1,3,2,0:T(8,128)(2,1)S(1)}, u32[]{:S(2)}, u32[]{:S(2)}) collective-permute-start(bf16[1,128,1,128]{1,3,2,0:T(8,128)(2,1)S(1)} %get-tuple-element.172), channel_id=1, source_target_pairs={{1,0},{2,1},{3,2},{5,4},{6,5},{7,6},{9,8},{10,9},{11,10},{13,12},{... | collective-permute-start | bytes 98312 | tf_op jit(solution)/shard_map/ppermute | solution.py:19
  89.5 5.7 %collective-permute-start.12 = (bf16[1,128,1,128]{1,3,2,0:T(8,128)(2,1)S(1)}, bf16[1,128,1,128]{1,3,2,0:T(8,128)(2,1)S(1)}, u32[]{:S(2)}, u32[]{:S(2)}) collective-permute-start(bf16[1,128,1,128]{1,3,2,0:T(8,128)(2,1)S(1)} %get-tuple-element.163), channel_id=1, source_target_pairs={{0,1},{1,2},{2,3},{4,5},{5,6},{6,7},{8,9},{9,10},{10,11},{12,13},{... | collective-permute-start | bytes 98312 | tf_op jit(solution)/shard_map/ppermute | solution.py:18
  100.4 6.0 %collective-permute-start.18 = (bf16[1,128,1,128]{1,3,2,0:T(8,128)(2,1)S(1)}, bf16[1,128,1,128]{1,3,2,0:T(8,128)(2,1)S(1)}, u32[]{:S(2)}, u32[]{:S(2)}) collective-permute-start(bf16[1,128,1,128]{1,3,2,0:T(8,128)(2,1)S(1)} %get-tuple-element.159), channel_id=1, source_target_pairs={{0,1},{1,2},{2,3},{4,5},{5,6},{6,7},{8,9},{9,10},{10,11},{12,13},{... | collective-permute-start | bytes 98312 | tf_op jit(solution)/shard_map/ppermute | solution.py:18
  110.5 9.3 %collective-permute-start.20 = (bf16[1,128,1,128]{1,3,2,0:T(8,128)(2,1)S(1)}, bf16[1,128,1,128]{1,3,2,0:T(8,128)(2,1)S(1)}, u32[]{:S(2)}, u32[]{:S(2)}) collective-permute-start(bf16[1,128,1,128]{1,3,2,0:T(8,128)(2,1)S(1)} %get-tuple-element.155), channel_id=1, source_target_pairs={{0,1},{1,2},{2,3},{4,5},{5,6},{6,7},{8,9},{9,10},{10,11},{12,13},{... | collective-permute-start | bytes 98312 | tf_op jit(solution)/shard_map/ppermute | solution.py:18
  114.6 5.2 %collective-permute-start.21 = (bf16[1,128,1,128]{1,3,2,0:T(8,128)(2,1)S(1)}, bf16[1,128,1,128]{1,3,2,0:T(8,128)(2,1)S(1)}, u32[]{:S(2)}, u32[]{:S(2)}) collective-permute-start(bf16[1,128,1,128]{1,3,2,0:T(8,128)(2,1)S(1)} %get-tuple-element.156), channel_id=1, source_target_pairs={{1,0},{2,1},{3,2},{5,4},{6,5},{7,6},{9,8},{10,9},{11,10},{13,12},{... | collective-permute-start | bytes 98312 | tf_op jit(solution)/shard_map/ppermute | solution.py:19
  126.8 7.8 %collective-permute-start.22 = (bf16[1,64,1,256]{3,2,1,0:T(2,128)(2,1)}, bf16[1,64,1,256]{3,2,1,0:T(2,128)(2,1)}, u32[]{:S(2)}, u32[]{:S(2)}) collective-permute-start(bf16[1,64,1,256]{3,2,1,0:T(2,128)(2,1)} %get-tuple-element.107), channel_id=1, source_target_pairs={{0,1},{1,2},{2,3},{4,5},{5,6},{6,7},{8,9},{9,10},{10,11},{12,13},{... | collective-permute-start | bytes 98312 | tf_op jit(solution)/shard_map/ppermute | solution.py:18
  130.5 5.0 %collective-permute-start.23 = (bf16[1,64,1,256]{3,2,1,0:T(2,128)(2,1)}, bf16[1,64,1,256]{3,2,1,0:T(2,128)(2,1)S(1)}, u32[]{:S(2)}, u32[]{:S(2)}) collective-permute-start(bf16[1,64,1,256]{3,2,1,0:T(2,128)(2,1)} %get-tuple-element.108), channel_id=1, source_target_pairs={{1,0},{2,1},{3,2},{5,4},{6,5},{7,6},{9,8},{10,9},{11,10},{13,12},{... | collective-permute-start | bytes 98312 | tf_op jit(solution)/shard_map/ppermute | solution.py:19
  141.2 4.8 %collective-permute-start.24 = (bf16[1,64,1,256]{3,2,1,0:T(2,128)(2,1)S(1)}, bf16[1,64,1,256]{3,2,1,0:T(2,128)(2,1)S(1)}, u32[]{:S(2)}, u32[]{:S(2)}) collective-permute-start(bf16[1,64,1,256]{3,2,1,0:T(2,128)(2,1)S(1)} %get-tuple-element.103), channel_id=1, source_target_pairs={{0,1},{1,2},{2,3},{4,5},{5,6},{6,7},{8,9},{9,10},{10,11},{12,13},{... | collective-permute-start | bytes 98312 | tf_op jit(solution)/shard_map/ppermute | solution.py:18
  144.6 4.2 %collective-permute-start.25 = (bf16[1,64,1,256]{3,2,1,0:T(2,128)(2,1)S(1)}, bf16[1,64,1,256]{3,2,1,0:T(2,128)(2,1)S(1)}, u32[]{:S(2)}, u32[]{:S(2)}) collective-permute-start(bf16[1,64,1,256]{3,2,1,0:T(2,128)(2,1)S(1)} %get-tuple-element.104), channel_id=1, source_target_pairs={{1,0},{2,1},{3,2},{5,4},{6,5},{7,6},{9,8},{10,9},{11,10},{13,12},{... | collective-permute-start | bytes 98312 | tf_op jit(solution)/shard_map/ppermute | solution.py:19
  151.6 7.8 %collective-permute-start.26 = (bf16[1,3,1,256]{3,1,2,0:T(4,128)(2,1)S(1)}, bf16[1,3,1,256]{3,1,2,0:T(4,128)(2,1)S(1)}, u32[]{:S(2)}, u32[]{:S(2)}) collective-permute-start(bf16[1,3,1,256]{3,1,2,0:T(4,128)(2,1)S(1)} %get-tuple-element.197), channel_id=1, source_target_pairs={{0,1},{1,2},{2,3},{4,5},{5,6},{6,7},{8,9},{9,10},{10,11},{12,13},{... | collective-permute-start | bytes 4616 | tf_op jit(solution)/shard_map/ppermute | solution.py:18
  (43 other events, 118.7 us)
